TPU v7x, 32 devices: a whole 2x2x4 slice. The times are simulated.
32 devices in a mesh: groups: 2 (over y), coef: 4 (over x, core), slab: 4 (over z).
Axes of the slice: x: 2, y: 2, z: 4, core: 2. Of those that a mesh axis runs over, the one named last changes fastest.
Arguments:
- coefficients: float32 [896, 32768], P('coef', ('groups', 'slab')), parts along dimension 1, may hold values from -6 to 6
- measured: float32 [16, 4, 64, 256], P('groups', 'slab'), parts along dimension 0, may hold values from -6 to 6
- ray_voxels: int32 [8, 64, 128], replicated, may hold values from 0 to 4095
- ray_weights: int32 [8, 64, 128], replicated, may hold values from 1 to 63
- angle_ids: int32 [8], replicated, may hold values from 0 to 15
- angle_table: bfloat16 [16, 896, 256], P(None, 'coef'), may hold values from -0.1875 to 0.1875
- harmonics: bfloat16 [896, 2048], P('coef'), may hold values from -0.1875 to 0.1875
Outputs:
- updated: float32 [896, 32768], P('coef', ('groups', 'slab')), parts along dimension 1
- residual: float32 [16, 4, 64, 256], P('groups', 'slab', None, 'coef'), parts along dimension 0
There are 2 independent parts, one for each index of `groups`. A program takes and returns all parts, laid end to end along the dimension named above; an argument that names none is the same for every part. Nothing has to cross between parts.
All inputs are finite; a program needn't handle non-finite values.
Results may differ from a plain program's by a relative error of at most 0.0034.
Values may be sent and summed in bfloat16 or wider, within the bound.
A program may use at most 64 MiB of HBM per device.

v0:
```python
import jax
import jax.numpy as jnp
from jax import lax
from jax.sharding import PartitionSpec as P

NG = 64


def build_matrix(ray_voxels, ray_weights):
    shape_all = ray_voxels.shape
    side_count = NG
    high_part = ray_voxels // side_count
    low_part = ray_voxels % side_count
    positions = jnp.arange(side_count, dtype=jnp.int32)
    values = (ray_weights.astype(jnp.float32) / 256.0).astype(jnp.bfloat16)
    high_table = jnp.where(
        high_part[..., None] == positions, values[..., None], jnp.zeros((), jnp.bfloat16)
    )
    low_table = (low_part[..., None] == positions).astype(jnp.bfloat16)
    high_flat = high_table.reshape(shape_all[0] * shape_all[1], shape_all[2], side_count)
    low_flat = low_table.reshape(shape_all[0] * shape_all[1], shape_all[2], side_count)
    product = lax.dot_general(
        high_flat, low_flat, (((1,), (1,)), ((0,), (0,))), preferred_element_type=jnp.float32
    )
    return product.astype(jnp.bfloat16).reshape(shape_all[0], shape_all[1], side_count * side_count)


def select_angles(angle_ids, angle_table):
    entries = angle_table.shape[0]
    onehot = (angle_ids[:, None] == jnp.arange(entries)[None, :]).astype(jnp.bfloat16)
    flat_table = angle_table.reshape(entries, -1)
    picked = jnp.dot(onehot, flat_table, preferred_element_type=jnp.float32)
    return picked.astype(jnp.bfloat16).reshape((angle_ids.shape[0],) + angle_table.shape[1:])


def body(coefficients, measured, ray_voxels, ray_weights, angle_ids, angle_table, harmonics):
    coef_local = coefficients.shape[0]
    layers = coefficients.shape[1] // (NG * NG)
    system_matrix = build_matrix(ray_voxels, ray_weights)
    chosen = select_angles(angle_ids, angle_table)
    coef_half = coefficients.astype(jnp.bfloat16)
    stacked_rows = coef_half.reshape(coef_local, layers, NG * NG)
    ray_totals = jnp.einsum(
        "dmj,hqj->dqmh", system_matrix, stacked_rows, preferred_element_type=jnp.float32
    ).astype(jnp.bfloat16)
    partial_value = jnp.einsum(
        "azrk,akc->azrc", ray_totals, chosen, preferred_element_type=jnp.float32
    )
    chan_width = measured.shape[3] // lax.axis_size("coef")
    chan_start = lax.axis_index("coef") * chan_width
    predicted = lax.psum_scatter(partial_value, "coef", scatter_dimension=3, tiled=True)
    residual = predicted - lax.dynamic_slice_in_dim(measured, chan_start, chan_width, 3)
    resid_half = residual.astype(jnp.bfloat16)
    backward_projection = jnp.einsum(
        "azrc,akc->azrk",
        lax.all_gather(resid_half, "coef", axis=3, tiled=True),
        chosen,
        preferred_element_type=jnp.float32,
    )
    backward_half = backward_projection.astype(jnp.bfloat16)
    misfit_gradient = jnp.einsum(
        "qci,qbcy->ybi", system_matrix, backward_half, preferred_element_type=jnp.float32
    )
    misfit_gradient = misfit_gradient.reshape(coef_local, layers * NG * NG)
    grid_rows = coef_half.reshape(coef_local, layers * NG, NG)
    blocks = lax.all_to_all(grid_rows, "coef", split_axis=1, concat_axis=0, tiled=True)
    width_all, row_span, item_count = blocks.shape
    flat_cols = blocks.reshape(width_all, row_span * item_count)
    orient_field = lax.dot_general(
        flat_cols,
        lax.all_gather(harmonics, "coef", axis=0, tiled=True),
        (((0,), (0,)), ((), ())),
        preferred_element_type=jnp.float32,
    )
    slope_half = (-jax.nn.sigmoid(-orient_field)).astype(jnp.bfloat16)
    reg_grad = lax.dot_general(
        lax.all_gather(harmonics, "coef", axis=0, tiled=True),
        slope_half,
        (((1,), (1,)), ((), ())),
        preferred_element_type=jnp.float32,
    )
    reg_grad = reg_grad.reshape(width_all, row_span, item_count)
    reg_grad = lax.all_to_all(reg_grad, "coef", split_axis=0, concat_axis=1, tiled=True)
    reg_grad = reg_grad.reshape(coef_local, layers * NG * NG)
    updated = coefficients - 0.5 * misfit_gradient - 0.5 * reg_grad
    return (updated, residual)


def solution(mesh):
    in_specs = (
        P("coef", ("groups", "slab")),
        P("groups", "slab", None, None),
        P(),
        P(),
        P(),
        P(None, "coef", None),
        P("coef", None),
    )
    out_specs = (P("coef", ("groups", "slab")), P("groups", "slab", None, "coef"))
    return jax.shard_map(body, mesh=mesh, in_specs=in_specs, out_specs=out_specs, check_vma=False)
```

profile of v0, /device:TPU:0, one launch (start us, length us, event | category | flops | bytes accessed | tf_op | source)
XLA Modules:
  0.0 229.0 jit_solution(1820628051874065335)
XLA Ops:
  7.2 0.0 all-gather.2.cloned.1.call-start
  7.2 0.7 all-gather.2.cloned.1.call-update
  7.9 2.3 convert_element_type.36
  10.2 0.0 copy-start
  10.2 0.0 copy-start.3
  10.2 0.0 copy-start.2
  10.2 2.5 %copy.37 = bf16[224,4096]{0,1:T(8,128)(2,1)} copy(bf16[224,4096]{1,0:T(8,128)(2,1)S(1)} %convert_element_type.36) | data formatting | bytes 3670016 | tf_op jit(solution)/shard_map/convert_element_type | solution.py:41
  12.7 0.0 copy-done
  12.7 4.2 %all-to-all-start = ((bf16[224,64,64]{0,2,1:T(8,128)(2,1)}), bf16[224,64,64]{0,2,1:T(8,128)(2,1)S(1)}, u32[]{:S(2)}, u32[]{:S(2)}) async-start(bf16[224,64,64]{0,2,1:T(8,128)(2,1)} %bitcast.58), calls=%async_computation | async-start | bytes 4194304 | tf_op jit(solution)/shard_map/all_to_all | solution.py:66
  16.9 0.0 copy-done.3
  17.0 0.0 copy-done.2
  17.0 0.2 add_select_fusion.1
  17.2 45.1 %all-to-all-done = bf16[224,64,64]{0,2,1:T(8,128)(2,1)S(1)} async-done(((bf16[224,64,64]{0,2,1:T(8,128)(2,1)}), bf16[224,64,64]{0,2,1:T(8,128)(2,1)S(1)}, u32[]{:S(2)}, u32[]{:S(2)}) %all-to-all-start) | async-done | bytes 1835040 | tf_op jit(solution)/shard_map/all_to_all | solution.py:66
  62.3 3.1 %copy.53 = bf16[224,4,16,64]{0,1,3,2:T(4,128)(2,1)} copy(bf16[224,4,16,64]{0,3,2,1:T(8,128)(2,1)S(1)} %bitcast.57) | data formatting | bytes 3670016 | tf_op jit(solution)/shard_map/all_to_all | solution.py:66
  65.3 3.9 %reshape.62 = bf16[896,1024]{0,1:T(8,128)(2,1)S(1)} reshape(bf16[4,224,16,64]{1,0,3,2:T(4,128)(2,1)} %bitcast.59) | data formatting | bytes 3670016 | tf_op jit(solution)/shard_map/reshape | solution.py:68
  69.3 0.0 all-gather.2.cloned.1.call-done
  69.3 13.8 %fusion.13 = f32[1024,896]{1,0:T(8,128)} fusion(bf16[896,2048]{1,0:T(8,128)(2,1)} %all-gather.2.cloned.1.call-done, bf16[896,1024]{0,1:T(8,128)(2,1)S(1)} %reshape.62), kind=kOutput, calls=%fused_computation.15 | convolution fusion | flops 7524581376 | bytes 9175040 | tf_op jit(solution)/shard_map/dot_general | solution.py:76
  83.1 7.7 %copy.39 = f32[896,16,64]{2,1,0:T(8,128)} copy(f32[896,16,64]{0,2,1:T(8,128)} %bitcast.64) | data formatting | bytes 7340032 | tf_op jit(solution)/shard_map/reshape | solution.py:82
  90.8 7.8 %reshape.68 = f32[4,1,229376]{2,1,0:T(1,128)} reshape(f32[896,16,64]{2,1,0:T(8,128)} %copy.39) | data formatting | bytes 7340032
  98.6 4.8 %all-to-all-start.1 = ((f32[4,1,229376]{2,1,0:T(1,128)}), f32[4,1,229376]{2,1,0:T(1,128)}, u32[]{:S(2)}, u32[]{:S(2)}) async-start(f32[4,1,229376]{2,1,0:T(1,128)} %reshape.68), calls=%async_computation.1 | async-start | bytes 7340032 | tf_op jit(solution)/shard_map/all_to_all | solution.py:83
  103.4 0.2 reduce-scatter.4.cloned.1.call-start
  103.6 6.6 %fusion.5 = bf16[512,64,64]{2,1,0:T(8,128)(2,1)} fusion(s32[512,128]{1,0:T(8,128)S(1)} %bitcast.68, s32[512,128]{1,0:T(8,128)S(1)} %bitcast.67, bf16[512,128]{1,0:T(8,128)(2,1)S(1)} %bitcast.70), kind=kOutput, calls=%fused_computation.8 | convolution fusion | flops 551550976 | bytes 4849664 | tf_op jit(solution)/shard_map/dot_general | solution.py:22
  110.3 12.0 %reshape.57 = bf16[8,64,4096]{2,1,0:T(8,128)(2,1)} reshape(bf16[512,64,64]{2,1,0:T(8,128)(2,1)} %fusion.5) | data formatting | bytes 8388608 | tf_op jit(solution)/shard_map/reshape | solution.py:25
  122.3 0.0 copy-start.5
  122.3 0.0 copy-start.1
  122.3 2.7 %copy.46 = bf16[2,8,224,256]{3,1,2,0:T(8,128)(2,1)S(1)} copy(bf16[2,8,224,256]{3,2,1,0:T(8,128)(2,1)} %bitcast.65) | data formatting | bytes 3670016
  125.0 0.0 copy-done.5
  125.0 0.5 convolution_convert_fusion
  125.4 0.0 copy-done.1
  125.5 3.8 %convolution_bitcast_fusion.1 = f32[8,1,64,256]{3,2,0,1:T(8,128)S(1)} fusion(bf16[8,224,256]{2,0,1:T(8,128)(2,1)S(1)} %bitcast.62, bf16[8,64,4096]{2,1,0:T(8,128)(2,1)} %reshape.57, bf16[224,4096]{1,0:T(8,128)(2,1)S(1)} %copy-done.1), kind=kOutput, calls=%fused_computation.20 | convolution fusion | flops 998359040 | bytes 7471104 | tf_op jit(solution)/shard_map/azrk,akc->azrc/dot_general | solution.py:46
  129.3 0.0 copy-start.4
  129.3 0.4 copy.44
  129.7 1.1 reshape.66
  130.8 0.0 reduce-scatter.4.cloned.1.call-update
  130.8 24.1 %reduce-scatter.4.cloned.1.call-done = f32[64,512]{1,0:T(8,128)} async-done(((f32[256,512]{1,0:T(8,128)}), f32[64,512]{1,0:T(8,128)}) %reduce-scatter.4.cloned.1.call-update) | async-done | bytes 131088
  155.0 1.0 reshape.67
  156.0 0.1 copy.45
  156.1 0.0 copy-done.4
  156.1 0.8 fusion.28
  157.0 0.1 copy.34
  157.1 6.8 %all_gather.7 = bf16[8,1,64,256]{2,0,1,3:T(8,128)(2,1)S(1)} all-gather(bf16[8,1,64,64]{2,0,1,3:T(8,128)(2,1)S(1)} %copy.34), channel_id=1, replica_groups=mesh['groups'=2,'coef'=4,'slab'=4] {'coef'}, dimensions={3}, use_global_device_ids=true | all-gather | bytes 327680 | tf_op jit(solution)/shard_map/all_gather | solution.py:56
  163.9 0.3 copy.35
  164.2 0.0 all-to-all-done.1
  164.3 0.5 broadcast.44
  164.8 13.6 %reduce = f32[4,229376]{1,0:T(4,128)} reduce(f32[4,1,229376]{2,1,0:T(1,128)} %all-to-all-done.1, f32[]{:T(128)} %broadcast.44), dimensions={1}, to_apply=%all_to_all.21.reduce_sub_computation | reduce | bytes 7340036 | tf_op jit(solution)/shard_map/all_to_all | solution.py:83
  178.4 8.4 %reshape.69 = f32[896,16,64]{2,1,0:T(8,128)} reshape(f32[4,229376]{1,0:T(4,128)} %reduce) | data formatting | bytes 7340032
  186.8 6.5 %copy.40 = f32[896,16,64]{0,2,1:T(8,128)} copy(f32[896,16,64]{2,1,0:T(8,128)} %reshape.69) | data formatting | bytes 7340032 | tf_op jit(solution)/shard_map/all_to_all | solution.py:83
  193.3 4.2 %broadcast_multiply_fusion = f32[896,16,64]{0,2,1:T(8,128)} fusion(f32[896,16,64]{0,2,1:T(8,128)} %copy.40), kind=kLoop, calls=%fused_computation.19 | loop fusion | flops 917504 | bytes 7340032 | tf_op jit(solution)/shard_map/mul | solution.py:85
  197.6 6.4 %mul.21 = f32[4,224,16,64]{1,0,3,2:T(4,128)} reshape(f32[896,16,64]{0,2,1:T(8,128)} %broadcast_multiply_fusion) | data formatting | bytes 7340032 | tf_op jit(solution)/shard_map/mul | solution.py:85
  204.0 5.0 %copy.41 = f32[224,4,16,64]{0,3,2,1:T(8,128)} copy(f32[224,4,16,64]{0,1,3,2:T(4,128)} %bitcast.55) | data formatting | bytes 7340032 | tf_op jit(solution)/shard_map/mul | solution.py:85
  209.0 5.5 %copy.42 = f32[224,4096]{1,0:T(8,128)} copy(f32[224,4096]{0,1:T(8,128)} %bitcast.56) | data formatting | bytes 7340032 | tf_op jit(solution)/shard_map/mul | solution.py:85
  214.4 7.8 %fusion.10 = f32[224,4096]{1,0:T(8,128)} fusion(f32[224,4096]{1,0:T(8,128)} %copy.42, f32[224,4096]{1,0:T(8,128)} %param.7, bf16[8,64,4096]{2,1,0:T(8,128)(2,1)} %reshape.57, bf16[8,224,256]{2,0,1:T(8,128)(2,1)S(1)} %bitcast.63, bf16[8,1,64,256]{3,2,0,1:T(8,128)(2,1)S(1)} %copy.35), kind=kOutput, calls=%fused_computation.12 | convolution fusion | flops 1001111552 | bytes 16384000 | tf_op jit(solution)/shard_map/qci,qbcy->ybi/dot_general | solution.py:61
  (1 shorter events, 0.0 us)
Async XLA Ops:
  7.2 62.1 %all-gather.2.cloned.1.call-start = ((), (), s32[]{:S(2)}) async-start(), calls=%async_computation.3 | async-start | bytes 4587520 | tf_op jit(solution)/shard_map/all_gather | solution.py:77
  10.2 2.5 %copy-start = (bf16[224,4096]{1,0:T(8,128)(2,1)}, bf16[224,4096]{1,0:T(8,128)(2,1)S(1)}, u32[]{:S(2)}) copy-start(bf16[224,4096]{1,0:T(8,128)(2,1)S(1)} %convert_element_type.36) | copy-start | bytes 5505028
  10.2 6.7 %copy-start.3 = (s32[8,64,128]{2,1,0:T(8,128)S(1)}, s32[8,64,128]{2,1,0:T(8,128)}, u32[]{:S(2)}) copy-start(s32[8,64,128]{2,1,0:T(8,128)} %param.10) | copy-start | bytes 786436
  10.2 6.8 %copy-start.2 = (s32[8,64,128]{2,1,0:T(8,128)S(1)}, s32[8,64,128]{2,1,0:T(8,128)}, u32[]{:S(2)}) copy-start(s32[8,64,128]{2,1,0:T(8,128)} %param.9) | copy-start | bytes 786436
  12.7 49.6 %all-to-all-start = ((bf16[224,64,64]{0,2,1:T(8,128)(2,1)}), bf16[224,64,64]{0,2,1:T(8,128)(2,1)S(1)}, u32[]{:S(2)}, u32[]{:S(2)}) async-start(bf16[224,64,64]{0,2,1:T(8,128)(2,1)} %bitcast.58), calls=%async_computation | async-start | bytes 4194304 | tf_op jit(solution)/shard_map/all_to_all | solution.py:66
  98.6 65.7 %all-to-all-start.1 = ((f32[4,1,229376]{2,1,0:T(1,128)}), f32[4,1,229376]{2,1,0:T(1,128)}, u32[]{:S(2)}, u32[]{:S(2)}) async-start(f32[4,1,229376]{2,1,0:T(1,128)} %reshape.68), calls=%async_computation.1 | async-start | bytes 7340032 | tf_op jit(solution)/shard_map/all_to_all | solution.py:83
  103.4 51.6 %reduce-scatter.4.cloned.1.call-start = ((), (), s32[]{:S(2)}) async-start(), calls=%async_computation.4 | async-start | bytes 655360
  122.3 2.7 %copy-start.5 = (s32[8]{0:T(128)S(1)}, s32[8]{0:T(128)}, u32[]{:S(2)}) copy-start(s32[8]{0:T(128)} %param.11) | copy-start | bytes 100
  122.3 3.1 %copy-start.1 = (bf16[224,4096]{1,0:T(8,128)(2,1)S(1)}, bf16[224,4096]{1,0:T(8,128)(2,1)}, u32[]{:S(2)}) copy-start(bf16[224,4096]{1,0:T(8,128)(2,1)} %copy-done) | copy-start | bytes 5505028
  129.3 26.8 %copy-start.4 = (f32[8,1,64,256]{3,2,1,0:T(8,128)S(1)}, f32[8,1,64,256]{3,2,1,0:T(8,128)}, u32[]{:S(2)}) copy-start(f32[8,1,64,256]{3,2,1,0:T(8,128)} %param.8) | copy-start | bytes 1572868
Sparse Core Ops, SparseCore 0:
  9.5 53.6 all-gather.1
  130.9 23.9 reduce-scatter.3
where the time goes:
time: 230 us; the launch traced here: 229 us
  local copies, waits for them, and re-layouts  75 us (33%)
  waiting for transfers between devices  69.9 us (30%)
  matrix products  32.5 us (14%)
  other arithmetic  21.3 us (9%)
  between operations  14.2 us (6%)
  starting transfers between devices  9.3 us (4%)
  blocking collectives  6.81 us (3%)
    all_to_all x1, waiting for transfers between devices, body(): lax.all_to_all(grid_rows, 'coef', split_axis=1, concat_axis=0, tiled=True)  45.1 us
    unnamed x3, waiting for transfers between devices  24.8 us
    unnamed x19, local copies, waits for them, and re-layouts  21.5 us
    mul x3, local copies, waits for them, and re-layouts, body(): updated = coefficients - 0.5 * misfit_gradient - 0.5 * reg_grad  16.9 us
    dot_general x1, matrix products, body(): lax.dot_general(lax.all_gather(harmonics, 'coef', axis=0, tiled=True), sl...  13.8 us
    all_to_all x1, other arithmetic, body(): lax.all_to_all(reg_grad, 'coef', split_axis=0, concat_axis=1, tiled=True)  13.6 us
    reshape x1, local copies, waits for them, and re-layouts, build_matrix(): product.astype(jnp.bfloat16)  12 us
    dot_general x1, matrix products, body(): jnp.einsum('qci,qbcy->ybi', system_matrix, backward_half, preferred_eleme...  7.78 us
  transfers between devices with their start and end apart: 4, of which 2 were waited for; matrix products, arithmetic and copies ran while one was open for 18% of the time, Pallas kernels for 0%

commit v1 on v0

--- a/solution.py
+++ b/solution.py
@@ -80,7 +80,10 @@
         preferred_element_type=jnp.float32,
     )
     reg_grad = reg_grad.reshape(width_all, row_span, item_count)
-    reg_grad = lax.all_to_all(reg_grad, "coef", split_axis=0, concat_axis=1, tiled=True)
+    reg_grad = jnp.concatenate(
+        lax.all_to_all(jnp.stack(jnp.split(reg_grad, lax.axis_size("coef"), axis=0)), "coef", 0, 0),
+        axis=1,
+    )
     reg_grad = reg_grad.reshape(coef_local, layers * NG * NG)
     updated = coefficients - 0.5 * misfit_gradient - 0.5 * reg_grad
     return (updated, residual)

time: 230 us -> 187 us (0.81)
  local copies, waits for them, and re-layouts: 75 us -> 41 us
  other arithmetic: 21.3 us -> 12.4 us
    unnamed x19, local copies, waits for them, and re-layouts: 21.5 us -> 5.32 us
    all_to_all x1 -> x0, other arithmetic: 13.6 us -> none  [body(): lax.all_to_all(reg_grad, 'coef', split_axis=0, concat_axis=1, tiled=True)]
    mul x3 -> x1, local copies, waits for them, and re-layouts: 16.9 us -> 5.46 us  [body(): updated = coefficients - 0.5 * misfit_gradient - 0.5 * reg_grad]
    split x0 -> x5, local copies, waits for them, and re-layouts: none -> 8.31 us  [body(): jnp.split(reg_grad, lax.axis_size('coef'), axis=0)]
    reshape x1 -> x0, local copies, waits for them, and re-layouts: 7.65 us -> none  [body(): reg_grad = reg_grad.reshape(width_all, row_span, item_count)]
    all_to_all x2 -> x0, local copies, waits for them, and re-layouts: 7.07 us -> none  [body(): lax.all_to_all(reg_grad, 'coef', split_axis=0, concat_axis=1, tiled=True)]
    another operation x0 -> x1, other arithmetic: none -> 3.55 us  [body(): jnp.stack(jnp.split(reg_grad, lax.axis_size('coef'), axis=0))]
  transfers between devices with their start and end apart: 4 -> 4, of which waited for: 2 -> 2; matrix products, arithmetic and copies ran while one was open for 18% -> 23% of each run, Pallas kernels for 0% -> 0%
where the time goes in v1:
time: 187 us; the launch traced here: 186 us
  waiting for transfers between devices  69.6 us (37%)
  local copies, waits for them, and re-layouts  41 us (22%)
  matrix products  32 us (17%)
  between operations  14.2 us (8%)
  other arithmetic  12.4 us (7%)
  starting transfers between devices  9.55 us (5%)
  blocking collectives  6.83 us (4%)
    all_to_all x1, waiting for transfers between devices, body(): lax.all_to_all(grid_rows, 'coef', split_axis=1, concat_axis=0, tiled=True)  44.4 us
    unnamed x3, waiting for transfers between devices  25.2 us
    dot_general x1, matrix products, body(): lax.dot_general(lax.all_gather(harmonics, 'coef', axis=0, tiled=True), sl...  13.3 us
    reshape x1, local copies, waits for them, and re-layouts, build_matrix(): product.astype(jnp.bfloat16)  12.1 us
    split x5, local copies, waits for them, and re-layouts, body(): jnp.split(reg_grad, lax.axis_size('coef'), axis=0)  8.31 us
    dot_general x1, matrix products, body(): jnp.einsum('qci,qbcy->ybi', system_matrix, backward_half, preferred_eleme...  7.78 us
    all_gather x1, blocking collectives, body(): lax.all_gather(resid_half, 'coef', axis=3, tiled=True)  6.83 us
    dot_general x1, matrix products, build_matrix(): lax.dot_general(high_flat, low_flat, (((1,), (1,)), ((0,), (0,))), prefer...  6.66 us
  transfers between devices with their start and end apart: 4, of which 2 were waited for; matrix products, arithmetic and copies ran while one was open for 23% of the time, Pallas kernels for 0%

profile of v1, /device:TPU:0, one launch (start us, length us, event | category | flops | bytes accessed | tf_op | source)
XLA Modules:
  0.0 185.6 jit_solution(11721875421787156479)
XLA Ops:
  7.2 0.0 all-gather.2.cloned.1.call-start
  7.2 0.7 all-gather.2.cloned.1.call-update
  7.9 2.3 %convert_element_type.36 = bf16[224,4096]{1,0:T(8,128)(2,1)S(1)} convert(f32[224,4096]{1,0:T(8,128)} %param.7) | non-fusion elementwise | flops 917504 | bytes 5505024 | tf_op jit(solution)/shard_map/convert_element_type | solution.py:41
  10.2 0.0 copy-start
  10.2 0.0 copy-start.4
  10.2 0.0 copy-start.2
  10.2 2.5 %copy.45 = bf16[224,4096]{0,1:T(8,128)(2,1)} copy(bf16[224,4096]{1,0:T(8,128)(2,1)S(1)} %convert_element_type.36) | data formatting | bytes 3670016 | tf_op jit(solution)/shard_map/convert_element_type | solution.py:41
  12.7 0.0 copy-done
  12.7 4.2 %all-to-all-start = ((bf16[224,64,64]{0,2,1:T(8,128)(2,1)}), bf16[224,64,64]{0,2,1:T(8,128)(2,1)S(1)}, u32[]{:S(2)}, u32[]{:S(2)}) async-start(bf16[224,64,64]{0,2,1:T(8,128)(2,1)} %bitcast.59), calls=%async_computation | async-start | bytes 4194304 | tf_op jit(solution)/shard_map/all_to_all | solution.py:66
  16.9 0.0 copy-done.4
  17.0 0.0 copy-done.2
  17.0 0.9 add_select_fusion.1
  17.9 44.4 %all-to-all-done = bf16[224,64,64]{0,2,1:T(8,128)(2,1)S(1)} async-done(((bf16[224,64,64]{0,2,1:T(8,128)(2,1)}), bf16[224,64,64]{0,2,1:T(8,128)(2,1)S(1)}, u32[]{:S(2)}, u32[]{:S(2)}) %all-to-all-start) | async-done | bytes 1835040 | tf_op jit(solution)/shard_map/all_to_all | solution.py:66
  62.3 3.1 %copy.62 = bf16[224,4,16,64]{0,1,3,2:T(4,128)(2,1)} copy(bf16[224,4,16,64]{0,3,2,1:T(8,128)(2,1)S(1)} %bitcast.58) | data formatting | bytes 3670016 | tf_op jit(solution)/shard_map/all_to_all | solution.py:66
  65.3 3.9 %reshape.65 = bf16[896,1024]{0,1:T(8,128)(2,1)S(1)} reshape(bf16[4,224,16,64]{1,0,3,2:T(4,128)(2,1)} %bitcast.60) | data formatting | bytes 3670016 | tf_op jit(solution)/shard_map/reshape | solution.py:68
  69.3 0.0 all-gather.2.cloned.1.call-done
  69.3 13.3 %fusion.14 = f32[896,1024]{1,0:T(8,128)} fusion(bf16[896,2048]{1,0:T(8,128)(2,1)} %all-gather.2.cloned.1.call-done, bf16[896,1024]{0,1:T(8,128)(2,1)S(1)} %reshape.65), kind=kOutput, calls=%fused_computation.19 | convolution fusion | flops 7524581376 | bytes 9175040 | tf_op jit(solution)/shard_map/dot_general | solution.py:76
  82.6 3.7 %fusion.34 = (f32[224,1024]{1,0:T(8,128)}, f32[224,1024]{1,0:T(8,128)S(1)}, f32[224,1024]{1,0:T(8,128)S(1)}, f32[224,1024]{1,0:T(8,128)}) fusion(f32[896,1024]{1,0:T(8,128)} %fusion.14), kind=kLoop, calls=%fused_computation.44 | loop fusion | bytes 7340032 | tf_op jit(solution)/shard_map/split | solution.py:84
  86.2 0.3 copy.50
  86.6 0.3 copy.49
  86.9 1.5 copy.48
  88.4 2.5 %copy.47 = f32[224,1024]{0,1:T(8,128)} copy(f32[224,1024]{1,0:T(8,128)} %get-tuple-element.10) | data formatting | bytes 1835008 | tf_op jit(solution)/shard_map/split | solution.py:84
  90.9 3.5 %pad_maximum_fusion = f32[4,224,16,64]{1,3,2,0:T(8,128)} fusion(f32[1,224,16,64]{1,3,2,0:T(8,128)S(1)} %bitcast.63, f32[1,224,16,64]{1,3,2,0:T(8,128)S(1)} %bitcast.64, f32[1,224,16,64]{1,3,2,0:T(8,128)S(1)} %bitcast.65, f32[1,224,16,64]{1,3,2,0:T(8,128)} %bitcast.66), kind=kLoop, calls=%fused_computation.13 | loop fusion | flops 2752512 | bytes 7340032 | tf_op jit(solution)/shard_map/stack | solution.py:84
  94.4 0.0 copy-start.3
  94.4 5.1 %all-to-all-start.1 = ((f32[4,224,16,64]{1,3,2,0:T(8,128)}), f32[4,224,16,64]{1,3,2,0:T(8,128)}, u32[]{:S(2)}, u32[]{:S(2)}) async-start(f32[4,224,16,64]{1,3,2,0:T(8,128)} %pad_maximum_fusion), calls=%async_computation.1 | async-start | bytes 8388608 | tf_op jit(solution)/shard_map/all_to_all | solution.py:84
  99.5 0.2 reduce-scatter.4.cloned.1.call-start
  99.7 0.0 copy-done.3
  99.7 6.7 %fusion.5 = bf16[512,64,64]{2,1,0:T(8,128)(2,1)} fusion(s32[512,128]{1,0:T(8,128)S(1)} %bitcast.72, s32[512,128]{1,0:T(8,128)S(1)} %bitcast.71, bf16[512,128]{1,0:T(8,128)(2,1)S(1)} %bitcast.74), kind=kOutput, calls=%fused_computation.8 | convolution fusion | flops 551550976 | bytes 4849664 | tf_op jit(solution)/shard_map/dot_general | solution.py:22
  106.4 0.0 copy-start.6
  106.4 12.1 %reshape.60 = bf16[8,64,4096]{2,1,0:T(8,128)(2,1)} reshape(bf16[512,64,64]{2,1,0:T(8,128)(2,1)} %fusion.5) | data formatting | bytes 8388608 | tf_op jit(solution)/shard_map/reshape | solution.py:25
  118.5 0.0 copy-start.1
  118.5 2.7 %copy.55 = bf16[2,8,224,256]{3,1,2,0:T(8,128)(2,1)S(1)} copy(bf16[2,8,224,256]{3,2,1,0:T(8,128)(2,1)} %bitcast.69) | data formatting | bytes 3670016
  121.1 0.0 copy-done.6
  121.1 0.5 convolution_convert_fusion
  121.6 0.0 copy-done.1
  121.6 3.8 %convolution_bitcast_fusion.1 = f32[8,1,64,256]{3,2,0,1:T(8,128)S(1)} fusion(bf16[8,224,256]{2,0,1:T(8,128)(2,1)S(1)} %bitcast.67, bf16[8,64,4096]{2,1,0:T(8,128)(2,1)} %reshape.60, bf16[224,4096]{1,0:T(8,128)(2,1)S(1)} %copy-done.1), kind=kOutput, calls=%fused_computation.22 | convolution fusion | flops 998359040 | bytes 7471104 | tf_op jit(solution)/shard_map/azrk,akc->azrc/dot_general | solution.py:46
  125.4 0.0 copy-start.5
  125.5 0.4 copy.53
  125.9 1.1 reshape.68
  126.9 0.0 reduce-scatter.4.cloned.1.call-update
  127.0 24.5 %reduce-scatter.4.cloned.1.call-done = f32[64,512]{1,0:T(8,128)} async-done(((f32[256,512]{1,0:T(8,128)}), f32[64,512]{1,0:T(8,128)}) %reduce-scatter.4.cloned.1.call-update) | async-done | bytes 131088
  151.4 1.0 reshape.69
  152.4 0.1 copy.54
  152.6 0.0 copy-done.5
  152.6 0.8 fusion.29
  153.4 0.1 copy.42
  153.6 6.8 %all_gather.7 = bf16[8,1,64,256]{2,0,1,3:T(8,128)(2,1)S(1)} all-gather(bf16[8,1,64,64]{2,0,1,3:T(8,128)(2,1)S(1)} %copy.42), channel_id=1, replica_groups=mesh['groups'=2,'coef'=4,'slab'=4] {'coef'}, dimensions={3}, use_global_device_ids=true | all-gather | bytes 327680 | tf_op jit(solution)/shard_map/all_gather | solution.py:56
  160.4 0.3 copy.43
  160.7 0.0 all-to-all-done.1
  160.8 4.7 %broadcast_multiply_fusion = f32[4,224,16,64]{1,3,2,0:T(8,128)} fusion(f32[4,224,16,64]{1,3,2,0:T(8,128)} %all-to-all-done.1), kind=kLoop, calls=%fused_computation.18 | loop fusion | flops 917504 | bytes 7340032 | tf_op jit(solution)/shard_map/mul | solution.py:88
  165.5 5.5 %copy.51 = f32[224,4096]{1,0:T(8,128)} copy(f32[224,4096]{0,1:T(8,128)} %bitcast.57) | data formatting | bytes 7340032 | tf_op jit(solution)/shard_map/mul | solution.py:88
  171.0 7.8 %fusion.10 = f32[224,4096]{1,0:T(8,128)} fusion(f32[224,4096]{1,0:T(8,128)} %copy.51, f32[224,4096]{1,0:T(8,128)} %param.7, bf16[8,64,4096]{2,1,0:T(8,128)(2,1)} %reshape.60, bf16[8,224,256]{2,0,1:T(8,128)(2,1)S(1)} %bitcast.68, bf16[8,1,64,256]{3,2,0,1:T(8,128)(2,1)S(1)} %copy.43), kind=kOutput, calls=%fused_computation.12 | convolution fusion | flops 1001111552 | bytes 16384000 | tf_op jit(solution)/shard_map/qci,qbcy->ybi/dot_general | solution.py:61
  (1 shorter events, 0.0 us)
Async XLA Ops:
  7.2 62.1 %all-gather.2.cloned.1.call-start = ((), (), s32[]{:S(2)}) async-start(), calls=%async_computation.3 | async-start | bytes 4587520 | tf_op jit(solution)/shard_map/all_gather | solution.py:77
  10.2 2.5 %copy-start = (bf16[224,4096]{1,0:T(8,128)(2,1)}, bf16[224,4096]{1,0:T(8,128)(2,1)S(1)}, u32[]{:S(2)}) copy-start(bf16[224,4096]{1,0:T(8,128)(2,1)S(1)} %convert_element_type.36) | copy-start | bytes 5505028
  10.2 6.7 %copy-start.4 = (s32[8,64,128]{2,1,0:T(8,128)S(1)}, s32[8,64,128]{2,1,0:T(8,128)}, u32[]{:S(2)}) copy-start(s32[8,64,128]{2,1,0:T(8,128)} %param.10) | copy-start | bytes 786436
  10.2 6.8 %copy-start.2 = (s32[8,64,128]{2,1,0:T(8,128)S(1)}, s32[8,64,128]{2,1,0:T(8,128)}, u32[]{:S(2)}) copy-start(s32[8,64,128]{2,1,0:T(8,128)} %param.9) | copy-start | bytes 786436
  12.7 49.6 %all-to-all-start = ((bf16[224,64,64]{0,2,1:T(8,128)(2,1)}), bf16[224,64,64]{0,2,1:T(8,128)(2,1)S(1)}, u32[]{:S(2)}, u32[]{:S(2)}) async-start(bf16[224,64,64]{0,2,1:T(8,128)(2,1)} %bitcast.59), calls=%async_computation | async-start | bytes 4194304 | tf_op jit(solution)/shard_map/all_to_all | solution.py:66
  94.4 5.3 %copy-start.3 = (s32[8,64,128]{2,1,0:T(8,128)S(1)}, s32[8,64,128]{2,1,0:T(8,128)}, u32[]{:S(2)}) copy-start(s32[8,64,128]{2,1,0:T(8,128)} %get-tuple-element.17) | copy-start | bytes 786436
  94.4 66.3 %all-to-all-start.1 = ((f32[4,224,16,64]{1,3,2,0:T(8,128)}), f32[4,224,16,64]{1,3,2,0:T(8,128)}, u32[]{:S(2)}, u32[]{:S(2)}) async-start(f32[4,224,16,64]{1,3,2,0:T(8,128)} %pad_maximum_fusion), calls=%async_computation.1 | async-start | bytes 8388608 | tf_op jit(solution)/shard_map/all_to_all | solution.py:84
  99.5 51.9 %reduce-scatter.4.cloned.1.call-start = ((), (), s32[]{:S(2)}) async-start(), calls=%async_computation.4 | async-start | bytes 655360
  106.4 14.7 %copy-start.6 = (s32[8]{0:T(128)S(1)}, s32[8]{0:T(128)}, u32[]{:S(2)}) copy-start(s32[8]{0:T(128)} %param.11) | copy-start | bytes 100
  118.5 3.1 %copy-start.1 = (bf16[224,4096]{1,0:T(8,128)(2,1)S(1)}, bf16[224,4096]{1,0:T(8,128)(2,1)}, u32[]{:S(2)}) copy-start(bf16[224,4096]{1,0:T(8,128)(2,1)} %copy-done) | copy-start | bytes 5505028
  125.4 27.1 %copy-start.5 = (f32[8,1,64,256]{3,2,1,0:T(8,128)S(1)}, f32[8,1,64,256]{3,2,1,0:T(8,128)}, u32[]{:S(2)}) copy-start(f32[8,1,64,256]{3,2,1,0:T(8,128)} %param.8) | copy-start | bytes 1572868
Sparse Core Ops, SparseCore 0:
  9.5 53.6 all-gather.1
  127.1 24.3 reduce-scatter.3
